TPU v7x, 512 devices: a whole 4x4x16 slice. The times are simulated.
512 devices in a mesh: dp: 8 (over y, x_lo), ctx: 64 (over z, x_hi, core).
Axes of the slice: x: 4 (x_hi: 2, x_lo: 2; x = x_hi * 2 + x_lo), y: 4, z: 16, core: 2. Of those that a mesh axis runs over, the one named last changes fastest.
Arguments:
- events: bfloat16 [8, 16384, 1024], P('dp', 'ctx'), may hold values from -6 to 6
- w_query: bfloat16 [1024, 512], replicated, may hold values from -0.1875 to 0.1875
- w_key: bfloat16 [1024, 512], replicated, may hold values from -0.1875 to 0.1875
- values: bfloat16 [8, 16384, 512], P('dp', 'ctx'), may hold values from -6 to 6
- grad_out: bfloat16 [8, 16384, 512], P('dp', 'ctx'), may hold values from -6 to 6
- lengths: int32 [8, 32], P('dp'), may hold values from 1 to 768, 16384 in all within a row
- stream_shift: int32 [8], P('dp'), may hold values from 0 to 16383
- block_keep: int32 [8, 128], P('dp'), may hold values 0 or 1
Outputs:
- attended: bfloat16 [8, 16384, 512], P('dp', 'ctx')
- grad_values: bfloat16 [8, 16384, 512], P('dp', 'ctx')
- grad_wq: bfloat16 [1024, 512], P('ctx')
- grad_wk: bfloat16 [1024, 512], P('ctx')
Inputs may be any that keep to these rules, and one draw needn't show every extreme that they name: The lengths of a stream sum to 16384; the longest is exactly 768.
All inputs are finite; a program needn't handle non-finite values. No bound on the sum of `block_keep` on one device may be relied on, other than what follows from the above.
Results may differ from a plain program's by a relative error of at most 0.011.
Values may be sent and summed in bfloat16 or wider, within the bound.
A program may use at most 64 MiB of HBM per device.

v0:
```python
import jax
import jax.numpy as jnp
from jax import lax
from jax.sharding import PartitionSpec as P

HD = 128
SPAN = 3
BLOCK = 128
MAXLEN = 768


def from_behind(value, axis, steps):
    count = lax.axis_size(axis)
    pairs = [(source, (source + steps) % count) for source in range(count)]
    return lax.ppermute(value, axis, pairs)


def tile_terms(query, grad, key, value, valid, scale, alpha):
    z = jnp.einsum("qhd,khd->hqk", query, key, preferred_element_type=jnp.float32) * alpha
    sig = jax.nn.sigmoid(z)
    weight = valid[None, :, :].astype(jnp.float32) * scale
    att = (z * sig * weight).astype(jnp.bfloat16)
    out = jnp.einsum("hqk,khd->qhd", att, value, preferred_element_type=jnp.float32)
    dprod = jnp.einsum("qhd,khd->hqk", grad, value, preferred_element_type=jnp.float32)
    dsc = (dprod * sig * (1.0 + z * (1.0 - sig)) * weight * alpha).astype(jnp.bfloat16)
    dquery = jnp.einsum("hqk,khd->qhd", dsc, key, preferred_element_type=jnp.float32)
    dkey = jnp.einsum("hqk,qhd->khd", dsc, query, preferred_element_type=jnp.float32)
    dvalue = jnp.einsum("hqk,qhd->khd", att, grad, preferred_element_type=jnp.float32)
    return (out, dquery, dkey, dvalue)


def body(events, w_query, w_key, values, grad_out, lengths, stream_shift, block_keep):
    rows = events.shape[1]
    features = w_query.shape[1]
    nheads = features // HD
    alpha = 1.0 / HD**0.5
    scale = 1.0 / MAXLEN**0.5
    local = events[0]
    queries = jnp.dot(local, w_query, preferred_element_type=jnp.float32).astype(jnp.bfloat16)
    keys = jnp.dot(local, w_key, preferred_element_type=jnp.float32).astype(jnp.bfloat16)
    queries = queries.reshape(rows, nheads, HD)
    keys = keys.reshape(rows, nheads, HD)
    vals = values[0].reshape(rows, nheads, HD)
    cotan = grad_out[0].reshape(rows, nheads, HD)
    cycle_size = lax.axis_size("ctx")
    myself = lax.axis_index("ctx")
    total = rows * cycle_size
    ends = jnp.cumsum(lengths[0])
    offset = stream_shift[0]
    keep = block_keep[0]
    blocks_all = jnp.arange(keep.shape[0], dtype=jnp.int32)
    within = jnp.arange(rows, dtype=jnp.int32)

    def describe(anchor):
        anchor = jnp.remainder(anchor, cycle_size)
        position = jnp.remainder(anchor * rows + within - offset, total)
        owner = jnp.sum((position[:, None] >= ends[None, :]).astype(jnp.int32), axis=1)
        which = position // BLOCK
        kept = (
            jnp.sum(jnp.where(which[:, None] == blocks_all[None, :], keep[None, :], 0), axis=1) > 0
        )
        return (position, owner, kept)

    zeros = jnp.zeros((rows, nheads, HD), jnp.float32)
    qinfo = describe(myself)
    moving = (keys, vals)
    carried = (zeros, zeros)
    out_acc = zeros
    dq_acc = zeros
    for step in range(SPAN + 1):
        if step > 0:
            moving = from_behind((moving[0], moving[1]), "ctx", 1)
            carried = (
                from_behind(carried[0].astype(jnp.bfloat16), "ctx", 1).astype(jnp.float32),
                from_behind(carried[1].astype(jnp.bfloat16), "ctx", 1).astype(jnp.float32),
            )
        kinfo = describe(myself - step)
        o, a, b, c = tile_terms(
            queries,
            cotan,
            moving[0],
            moving[1],
            (qinfo[1][:, None] == kinfo[1][None, :])
            & (kinfo[0][None, :] <= qinfo[0][:, None])
            & kinfo[2][None, :],
            scale,
            alpha,
        )
        out_acc = out_acc + o
        dq_acc = dq_acc + a
        carried = (carried[0] + b, carried[1] + c)
    carried = (
        from_behind(carried[0].astype(jnp.bfloat16), "ctx", -SPAN).astype(jnp.float32),
        from_behind(carried[1].astype(jnp.bfloat16), "ctx", -SPAN).astype(jnp.float32),
    )
    dk_acc, dv_acc = carried
    attended = out_acc.reshape(1, rows, features).astype(jnp.bfloat16)
    grad_values = dv_acc.reshape(1, rows, features).astype(jnp.bfloat16)
    dq_b = dq_acc.reshape(rows, features).astype(jnp.bfloat16)
    dk_b = dk_acc.reshape(rows, features).astype(jnp.bfloat16)
    joined = jnp.concatenate([dq_b, dk_b], axis=1)
    width_rows = local.shape[1]
    share = width_rows // cycle_size
    terms = jnp.einsum("rd,rf->df", local, joined, preferred_element_type=jnp.float32)
    summed = lax.psum(terms, ("dp", "ctx"))
    mine = lax.dynamic_slice_in_dim(summed, myself * share, share, 0)
    grad_wq = mine[:, :features].astype(jnp.bfloat16)
    grad_wk = mine[:, features:].astype(jnp.bfloat16)
    return (attended, grad_values, grad_wq, grad_wk)


def solution(mesh):
    placed = (
        P("dp", "ctx", None),
        P(),
        P(),
        P("dp", "ctx", None),
        P("dp", "ctx", None),
        P("dp", None),
        P("dp"),
        P("dp", None),
    )
    return jax.shard_map(
        body,
        mesh=mesh,
        in_specs=placed,
        out_specs=(P("dp", "ctx", None), P("dp", "ctx", None), P("ctx", None), P("ctx", None)),
        check_vma=False,
    )
```

profile of v0, /device:TPU:7, one launch (start us, length us, event | category | flops | bytes accessed | tf_op | source)
XLA Modules:
  0.0 291.1 jit_solution(15227647348382941098)
XLA Ops:
  0.6 1.2 copy.87
  1.8 4.9 %collective-permute-start.1 = (bf16[256,4,128]{0,2,1:T(8,128)(2,1)S(1)}, bf16[256,4,128]{0,2,1:T(8,128)(2,1)S(1)}, u32[]{:S(2)}, u32[]{:S(2)}) collective-permute-start(bf16[256,4,128]{0,2,1:T(8,128)(2,1)S(1)} %bitcast.101), channel_id=1, source_target_pairs={{0,1},{1,2},{2,3},{3,4},{4,5},{5,6},{6,7},{7,8},{8,9},{9,10},{10,1... | collective-permute-start | bytes 786440 | tf_op jit(solution)/shard_map/ppermute | solution.py:15
  6.8 1.5 fusion.20
  8.3 0.7 copy.157
  9.0 1.9 collective-permute-start
  11.7 1.0 select_reduce_fusion
  12.8 0.7 copy.86
  13.7 1.0 reshape_squeeze.7
  14.8 1.8 convolution_convert_fusion.3
  16.8 1.2 and_select_fusion
  18.0 0.5 multiply_convert_fusion.3
  18.6 0.5 fusion.15
  19.1 1.0 fusion.19
  20.1 4.1 %collective-permute-start.10 = (bf16[256,4,128]{0,2,1:T(8,128)(2,1)}, bf16[256,4,128]{0,2,1:T(8,128)(2,1)}, u32[]{:S(2)}, u32[]{:S(2)}) collective-permute-start(bf16[256,4,128]{0,2,1:T(8,128)(2,1)} %fusion.19), channel_id=1, source_target_pairs={{0,1},{1,2},{2,3},{3,4},{4,5},{5,6},{6,7},{7,8},{8,9},{9,10},{10,1... | collective-permute-start | bytes 786440 | tf_op jit(solution)/shard_map/ppermute | solution.py:15
  24.2 1.1 fusion.18
  25.3 1.9 collective-permute-start.6
  27.8 1.6 multiply_convert_fusion.2
  30.0 1.2 add_convert_fusion.2
  31.2 4.8 %collective-permute-start.11 = (bf16[256,4,128]{0,2,1:T(8,128)(2,1)S(1)}, bf16[256,4,128]{0,2,1:T(8,128)(2,1)S(1)}, u32[]{:S(2)}, u32[]{:S(2)}) collective-permute-start(bf16[256,4,128]{0,2,1:T(8,128)(2,1)S(1)} %add_convert_fusion.2), channel_id=1, source_target_pairs={{0,1},{1,2},{2,3},{3,4},{4,5},{5,6},{6,7},{7,8},{8,9},{9,10},{10,1... | collective-permute-start | bytes 786440 | tf_op jit(solution)/shard_map/ppermute | solution.py:15
  36.0 1.3 add_convert_fusion.5
  37.3 1.9 collective-permute-start.7
  39.2 4.1 %collective-permute-start.3 = (bf16[256,4,128]{0,2,1:T(8,128)(2,1)S(1)}, bf16[256,4,128]{0,2,1:T(8,128)(2,1)S(1)}, u32[]{:S(2)}, u32[]{:S(2)}) collective-permute-start(bf16[256,4,128]{0,2,1:T(8,128)(2,1)S(1)} %collective-permute-done.1), channel_id=1, source_target_pairs={{0,1},{1,2},{2,3},{3,4},{4,5},{5,6},{6,7},{7,8},{8,9},{9,10},{10,1... | collective-permute-start | bytes 786440 | tf_op jit(solution)/shard_map/ppermute | solution.py:15
  43.4 1.9 collective-permute-start.2
  45.6 1.3 convolution_add_fusion.2
  46.9 2.7 collective-permute-done.2
  49.6 0.5 multiply_convert_fusion.1
  50.2 0.5 fusion.13
  51.0 6.7 %collective-permute-start.12 = (bf16[256,4,128]{0,2,1:T(8,128)(2,1)S(1)}, bf16[256,4,128]{0,2,1:T(8,128)(2,1)S(1)}, u32[]{:S(2)}, u32[]{:S(2)}) collective-permute-start(bf16[256,4,128]{0,2,1:T(8,128)(2,1)S(1)} %add_convert_fusion.1), channel_id=1, source_target_pairs={{0,1},{1,2},{2,3},{3,4},{4,5},{5,6},{6,7},{7,8},{8,9},{9,10},{10,1... | collective-permute-start | bytes 786440 | tf_op jit(solution)/shard_map/ppermute | solution.py:15
  58.1 0.7 add_convert_fusion.4
  58.8 1.9 collective-permute-start.8
  60.7 3.9 %collective-permute-start.5 = (bf16[256,4,128]{0,2,1:T(8,128)(2,1)S(1)}, bf16[256,4,128]{0,2,1:T(8,128)(2,1)S(1)}, u32[]{:S(2)}, u32[]{:S(2)}) collective-permute-start(bf16[256,4,128]{0,2,1:T(8,128)(2,1)S(1)} %collective-permute-done.3), channel_id=1, source_target_pairs={{0,1},{1,2},{2,3},{3,4},{4,5},{5,6},{6,7},{7,8},{8,9},{9,10},{10,1... | collective-permute-start | bytes 786440 | tf_op jit(solution)/shard_map/ppermute | solution.py:15
  64.6 1.9 collective-permute-start.4
  67.2 3.5 %collective-permute-done.4 = bf16[256,4,128]{2,0,1:T(8,128)(2,1)S(1)} collective-permute-done((bf16[256,4,128]{2,0,1:T(8,128)(2,1)S(1)}, bf16[256,4,128]{2,0,1:T(8,128)(2,1)S(1)}, u32[]{:S(2)}, u32[]{:S(2)}) %collective-permute-start.4) | collective-permute-done | bytes 262176 | tf_op jit(solution)/shard_map/ppermute | solution.py:15
  70.7 0.5 multiply_convert_fusion
  71.4 0.5 fusion.12
  72.2 1.0 fusion.16
  73.2 0.8 add_convert_fusion
  74.0 1.8 copy.117
  75.8 9.6 %collective-permute-start.13 = (bf16[256,4,128]{0,2,1:T(8,128)(2,1)}, bf16[256,4,128]{0,2,1:T(8,128)(2,1)}, u32[]{:S(2)}, u32[]{:S(2)}) collective-permute-start(bf16[256,4,128]{0,2,1:T(8,128)(2,1)} %add_convert_fusion), channel_id=1, source_target_pairs={{0,61},{1,62},{2,63},{3,0},{4,1},{5,2},{6,3},{7,4},{8,5},{9,6},{10... | collective-permute-start | bytes 786440 | tf_op jit(solution)/shard_map/ppermute | solution.py:15
  85.8 1.0 add_convert_fusion.3
  86.8 2.1 collective-permute-start.9
  88.9 1.3 fusion.17
  90.2 4.3 %collective-permute-done.9 = bf16[256,4,128]{2,0,1:T(8,128)(2,1)S(1)} collective-permute-done((bf16[256,4,128]{2,0,1:T(8,128)(2,1)S(1)}, bf16[256,4,128]{2,0,1:T(8,128)(2,1)S(1)}, u32[]{:S(2)}, u32[]{:S(2)}) %collective-permute-start.9) | collective-permute-done | bytes 262176 | tf_op jit(solution)/shard_map/ppermute | solution.py:15
  94.6 0.8 copy.118
  95.5 3.6 %convolution_bitcast_fusion = f32[1024,1024]{0,1:T(8,128)} fusion(bf16[256,512]{0,1:T(8,128)(2,1)} %bitcast.18, bf16[256,512]{0,1:T(8,128)(2,1)S(1)} %bitcast.104, bf16[1,256,1024]{2,1,0:T(8,128)(2,1)S(1)} %copy-done.1), kind=kOutput, calls=%fused_computation | convolution fusion | flops 537919488 | bytes 5242880 | tf_op jit(solution)/shard_map/rd,rf->df/dot_general | solution.py:104
  99.1 190.5 %all-reduce.1 = bf16[1024,1024]{0,1:T(8,128)(2,1)S(1)} all-reduce(f32[1024,1024]{0,1:T(8,128)} %convolution_bitcast_fusion), channel_id=1, replica_groups=mesh['dp'=8,'ctx'=64] {'dp','ctx'}, use_global_device_ids=true, to_apply=%region_9.10 | all-reduce | flops 1048576 | bytes 6291456 | tf_op jit(solution)/shard_map/psum | solution.py:105
  289.8 0.7 copy.120
  290.5 0.7 copy.119
  (49 shorter events, 4.3 us)
Async XLA Ops:
  0.6 6.2 %copy-start = (bf16[1024,512]{1,0:T(8,128)(2,1)S(1)}, bf16[1024,512]{1,0:T(8,128)(2,1)}, u32[]{:S(2)}) copy-start(bf16[1024,512]{1,0:T(8,128)(2,1)} %param.10) | copy-start | bytes 3145732
  1.8 27.6 %collective-permute-start.1 = (bf16[256,4,128]{0,2,1:T(8,128)(2,1)S(1)}, bf16[256,4,128]{0,2,1:T(8,128)(2,1)S(1)}, u32[]{:S(2)}, u32[]{:S(2)}) collective-permute-start(bf16[256,4,128]{0,2,1:T(8,128)(2,1)S(1)} %bitcast.101), channel_id=1, source_target_pairs={{0,1},{1,2},{2,3},{3,4},{4,5},{5,6},{6,7},{7,8},{8,9},{9,10},{10,1... | collective-permute-start | bytes 786440 | tf_op jit(solution)/shard_map/ppermute | solution.py:15
  9.0 18.8 %collective-permute-start = (bf16[256,4,128]{2,0,1:T(8,128)(2,1)}, bf16[256,4,128]{2,0,1:T(8,128)(2,1)}, u32[]{:S(2)}, u32[]{:S(2)}) collective-permute-start(bf16[256,4,128]{2,0,1:T(8,128)(2,1)} %bitcast.88), channel_id=1, source_target_pairs={{0,1},{1,2},{2,3},{3,4},{4,5},{5,6},{6,7},{7,8},{8,9},{9,10},{10,1... | collective-permute-start | bytes 786440 | tf_op jit(solution)/shard_map/ppermute | solution.py:15
  20.1 9.9 %collective-permute-start.10 = (bf16[256,4,128]{0,2,1:T(8,128)(2,1)}, bf16[256,4,128]{0,2,1:T(8,128)(2,1)}, u32[]{:S(2)}, u32[]{:S(2)}) collective-permute-start(bf16[256,4,128]{0,2,1:T(8,128)(2,1)} %fusion.19), channel_id=1, source_target_pairs={{0,1},{1,2},{2,3},{3,4},{4,5},{5,6},{6,7},{7,8},{8,9},{9,10},{10,1... | collective-permute-start | bytes 786440 | tf_op jit(solution)/shard_map/ppermute | solution.py:15
  25.3 10.7 %collective-permute-start.6 = (bf16[256,4,128]{2,0,1:T(8,128)(2,1)}, bf16[256,4,128]{2,0,1:T(8,128)(2,1)}, u32[]{:S(2)}, u32[]{:S(2)}) collective-permute-start(bf16[256,4,128]{2,0,1:T(8,128)(2,1)} %fusion.18), channel_id=1, source_target_pairs={{0,1},{1,2},{2,3},{3,4},{4,5},{5,6},{6,7},{7,8},{8,9},{9,10},{10,1... | collective-permute-start | bytes 786440 | tf_op jit(solution)/shard_map/ppermute | solution.py:15
  27.5 1.9 copy-start.4
  30.0 19.6 %copy-start.3 = (f32[256,256]{1,0:T(8,128)S(1)}, f32[256,256]{1,0:T(8,128)}, u32[]{:S(2)}) copy-start(f32[256,256]{1,0:T(8,128)} %get-tuple-element.27) | copy-start | bytes 786436
  31.2 19.7 %collective-permute-start.11 = (bf16[256,4,128]{0,2,1:T(8,128)(2,1)S(1)}, bf16[256,4,128]{0,2,1:T(8,128)(2,1)S(1)}, u32[]{:S(2)}, u32[]{:S(2)}) collective-permute-start(bf16[256,4,128]{0,2,1:T(8,128)(2,1)S(1)} %add_convert_fusion.2), channel_id=1, source_target_pairs={{0,1},{1,2},{2,3},{3,4},{4,5},{5,6},{6,7},{7,8},{8,9},{9,10},{10,1... | collective-permute-start | bytes 786440 | tf_op jit(solution)/shard_map/ppermute | solution.py:15
  37.3 20.8 %collective-permute-start.7 = (bf16[256,4,128]{2,0,1:T(8,128)(2,1)S(1)}, bf16[256,4,128]{2,0,1:T(8,128)(2,1)S(1)}, u32[]{:S(2)}, u32[]{:S(2)}) collective-permute-start(bf16[256,4,128]{2,0,1:T(8,128)(2,1)S(1)} %add_convert_fusion.5), channel_id=1, source_target_pairs={{0,1},{1,2},{2,3},{3,4},{4,5},{5,6},{6,7},{7,8},{8,9},{9,10},{10,1... | collective-permute-start | bytes 786440 | tf_op jit(solution)/shard_map/ppermute | solution.py:15
  39.2 10.9 %collective-permute-start.3 = (bf16[256,4,128]{0,2,1:T(8,128)(2,1)S(1)}, bf16[256,4,128]{0,2,1:T(8,128)(2,1)S(1)}, u32[]{:S(2)}, u32[]{:S(2)}) collective-permute-start(bf16[256,4,128]{0,2,1:T(8,128)(2,1)S(1)} %collective-permute-done.1), channel_id=1, source_target_pairs={{0,1},{1,2},{2,3},{3,4},{4,5},{5,6},{6,7},{7,8},{8,9},{9,10},{10,1... | collective-permute-start | bytes 786440 | tf_op jit(solution)/shard_map/ppermute | solution.py:15
  43.4 6.2 %collective-permute-start.2 = (bf16[256,4,128]{2,0,1:T(8,128)(2,1)}, bf16[256,4,128]{2,0,1:T(8,128)(2,1)S(1)}, u32[]{:S(2)}, u32[]{:S(2)}) collective-permute-start(bf16[256,4,128]{2,0,1:T(8,128)(2,1)} %collective-permute-done), channel_id=1, source_target_pairs={{0,1},{1,2},{2,3},{3,4},{4,5},{5,6},{6,7},{7,8},{8,9},{9,10},{10,1... | collective-permute-start | bytes 786440 | tf_op jit(solution)/shard_map/ppermute | solution.py:15
  50.7 20.0 %copy-start.2 = (f32[256,256]{1,0:T(8,128)S(1)}, f32[256,256]{1,0:T(8,128)}, u32[]{:S(2)}) copy-start(f32[256,256]{1,0:T(8,128)} %get-tuple-element.26) | copy-start | bytes 786436
  51.0 22.2 %collective-permute-start.12 = (bf16[256,4,128]{0,2,1:T(8,128)(2,1)S(1)}, bf16[256,4,128]{0,2,1:T(8,128)(2,1)S(1)}, u32[]{:S(2)}, u32[]{:S(2)}) collective-permute-start(bf16[256,4,128]{0,2,1:T(8,128)(2,1)S(1)} %add_convert_fusion.1), channel_id=1, source_target_pairs={{0,1},{1,2},{2,3},{3,4},{4,5},{5,6},{6,7},{7,8},{8,9},{9,10},{10,1... | collective-permute-start | bytes 786440 | tf_op jit(solution)/shard_map/ppermute | solution.py:15
  58.8 26.9 %collective-permute-start.8 = (bf16[256,4,128]{2,0,1:T(8,128)(2,1)}, bf16[256,4,128]{2,0,1:T(8,128)(2,1)}, u32[]{:S(2)}, u32[]{:S(2)}) collective-permute-start(bf16[256,4,128]{2,0,1:T(8,128)(2,1)} %add_convert_fusion.4), channel_id=1, source_target_pairs={{0,1},{1,2},{2,3},{3,4},{4,5},{5,6},{6,7},{7,8},{8,9},{9,10},{10,1... | collective-permute-start | bytes 786440 | tf_op jit(solution)/shard_map/ppermute | solution.py:15
  60.7 10.5 %collective-permute-start.5 = (bf16[256,4,128]{0,2,1:T(8,128)(2,1)S(1)}, bf16[256,4,128]{0,2,1:T(8,128)(2,1)S(1)}, u32[]{:S(2)}, u32[]{:S(2)}) collective-permute-start(bf16[256,4,128]{0,2,1:T(8,128)(2,1)S(1)} %collective-permute-done.3), channel_id=1, source_target_pairs={{0,1},{1,2},{2,3},{3,4},{4,5},{5,6},{6,7},{7,8},{8,9},{9,10},{10,1... | collective-permute-start | bytes 786440 | tf_op jit(solution)/shard_map/ppermute | solution.py:15
  64.6 6.1 %collective-permute-start.4 = (bf16[256,4,128]{2,0,1:T(8,128)(2,1)S(1)}, bf16[256,4,128]{2,0,1:T(8,128)(2,1)S(1)}, u32[]{:S(2)}, u32[]{:S(2)}) collective-permute-start(bf16[256,4,128]{2,0,1:T(8,128)(2,1)S(1)} %collective-permute-done.2), channel_id=1, source_target_pairs={{0,1},{1,2},{2,3},{3,4},{4,5},{5,6},{6,7},{7,8},{8,9},{9,10},{10,1... | collective-permute-start | bytes 786440 | tf_op jit(solution)/shard_map/ppermute | solution.py:15
  70.7 0.7 copy-start.5
  72.2 23.3 %copy-start.1 = (bf16[1,256,1024]{2,1,0:T(8,128)(2,1)S(1)}, bf16[1,256,1024]{2,1,0:T(8,128)(2,1)}, u32[]{:S(2)}) copy-start(bf16[1,256,1024]{2,1,0:T(8,128)(2,1)} %param.8) | copy-start | bytes 1572868
  75.8 19.7 %collective-permute-start.13 = (bf16[256,4,128]{0,2,1:T(8,128)(2,1)}, bf16[256,4,128]{0,2,1:T(8,128)(2,1)}, u32[]{:S(2)}, u32[]{:S(2)}) collective-permute-start(bf16[256,4,128]{0,2,1:T(8,128)(2,1)} %add_convert_fusion), channel_id=1, source_target_pairs={{0,61},{1,62},{2,63},{3,0},{4,1},{5,2},{6,3},{7,4},{8,5},{9,6},{10... | collective-permute-start | bytes 786440 | tf_op jit(solution)/shard_map/ppermute | solution.py:15
  86.8 7.7 %collective-permute-start.9 = (bf16[256,4,128]{2,0,1:T(8,128)(2,1)S(1)}, bf16[256,4,128]{2,0,1:T(8,128)(2,1)S(1)}, u32[]{:S(2)}, u32[]{:S(2)}) collective-permute-start(bf16[256,4,128]{2,0,1:T(8,128)(2,1)S(1)} %add_convert_fusion.3), channel_id=1, source_target_pairs={{0,61},{1,62},{2,63},{3,0},{4,1},{5,2},{6,3},{7,4},{8,5},{9,6},{10... | collective-permute-start | bytes 786440 | tf_op jit(solution)/shard_map/ppermute | solution.py:15
where the time goes:
time: 292 us; the launch traced here: 291 us
  blocking collectives  191 us (65%)
  starting transfers between devices  51.7 us (18%)
  matrix products  23 us (8%)
  waiting for transfers between devices  10.6 us (4%)
  local copies, waits for them, and re-layouts  8.31 us (3%)
  other arithmetic  5.18 us (2%)
    psum x1, blocking collectives, body(): summed = lax.psum(terms, ('dp', 'ctx'))  191 us
    ppermute x14, starting transfers between devices, from_behind(): return lax.ppermute(value, axis, pairs)  51.7 us
    ppermute x14, waiting for transfers between devices, from_behind(): return lax.ppermute(value, axis, pairs)  10.6 us
  transfers between devices with their start and end apart: 14, of which 3 were waited for; matrix products, arithmetic and copies ran while one was open for 10% of the time, Pallas kernels for 0%

commit v1 on v0

--- a/solution.py
+++ b/solution.py
@@ -102,7 +102,8 @@
     width_rows = local.shape[1]
     share = width_rows // cycle_size
     terms = jnp.einsum("rd,rf->df", local, joined, preferred_element_type=jnp.float32)
-    summed = lax.psum(terms, ("dp", "ctx"))
+    one_axis = lax.psum(terms, "dp")
+    summed = lax.psum(one_axis, "ctx")
     mine = lax.dynamic_slice_in_dim(summed, myself * share, share, 0)
     grad_wq = mine[:, :features].astype(jnp.bfloat16)
     grad_wk = mine[:, features:].astype(jnp.bfloat16)

time: 292 us -> 614 us (2.10); the launches traced: 291 us -> 603 us
  waiting for transfers between devices: 10.6 us -> 181 us
  blocking collectives: 191 us -> 298 us
  starting transfers between devices: 51.7 us -> 77.7 us
  between operations: 1.85 us -> 15.3 us
    psum x0 -> x1, waiting for transfers between devices: none -> 156 us  [body(): one_axis = lax.psum(terms, 'dp')]
    psum x1, blocking collectives: 191 us -> 298 us  [body(): summed = lax.psum(one_axis, 'ctx')]
    ppermute x14, starting transfers between devices: 51.7 us -> 77.6 us  [from_behind(): return lax.ppermute(value, axis, pairs)]
    ppermute x14, waiting for transfers between devices: 10.6 us -> 24.9 us  [from_behind(): return lax.ppermute(value, axis, pairs)]
  transfers between devices with their start and end apart: 14 -> 15, of which waited for: 3 -> 9; matrix products, arithmetic and copies ran while one was open for 10% -> 4% of each run, Pallas kernels for 0% -> 0%
where the time goes in v1:
time: 614 us; the launch traced here: 603 us
  blocking collectives  298 us (49%)
  waiting for transfers between devices  181 us (29%)
  starting transfers between devices  77.7 us (13%)
  matrix products  21.6 us (4%)
  between operations  15.3 us (2%)
  local copies, waits for them, and re-layouts  7.24 us (1%)
    psum x1, blocking collectives, body(): summed = lax.psum(one_axis, 'ctx')  298 us
    psum x1, waiting for transfers between devices, body(): one_axis = lax.psum(terms, 'dp')  156 us
    ppermute x14, starting transfers between devices, from_behind(): return lax.ppermute(value, axis, pairs)  77.6 us
    ppermute x14, waiting for transfers between devices, from_behind(): return lax.ppermute(value, axis, pairs)  24.9 us
  transfers between devices with their start and end apart: 15, of which 9 were waited for; matrix products, arithmetic and copies ran while one was open for 4% of the time, Pallas kernels for 0%

profile of v1, /device:TPU:7, one launch (start us, length us, event | category | flops | bytes accessed | tf_op | source)
XLA Modules:
  0.0 603.2 jit_solution(7987297032252595614)
XLA Ops:
  7.2 1.2 copy.87
  8.4 4.9 collective-permute-start.1
  13.4 1.5 fusion.20
  14.9 0.7 copy.157
  15.6 1.9 collective-permute-start
  18.3 1.0 select_reduce_fusion
  19.4 0.7 copy.86
  20.3 1.0 reshape_squeeze.7
  21.3 1.8 convolution_convert_fusion.3
  23.7 1.4 multiply_convert_fusion.3
  25.9 4.1 collective-permute-start.10
  30.4 1.5 multiply_convert_fusion.2
  31.9 0.5 fusion.14
  32.4 0.9 collective-permute-done.10
  33.6 6.8 %collective-permute-start.11 = (bf16[256,4,128]{0,2,1:T(8,128)(2,1)S(1)}, bf16[256,4,128]{0,2,1:T(8,128)(2,1)S(1)}, u32[]{:S(2)}, u32[]{:S(2)}) collective-permute-start(bf16[256,4,128]{0,2,1:T(8,128)(2,1)S(1)} %add_convert_fusion.2), channel_id=1, source_target_pairs={{0,1},{1,2},{2,3},{3,4},{4,5},{5,6},{6,7},{7,8},{8,9},{9,10},{10,1... | collective-permute-start | bytes 786440 | tf_op jit(solution)/shard_map/ppermute | solution.py:15
  40.4 1.9 collective-permute-start.3
  42.3 3.9 collective-permute-start.2
  46.2 1.3 convolution_add_fusion.2
  47.5 2.3 collective-permute-done.2
  49.8 0.5 multiply_convert_fusion.1
  50.4 0.5 fusion.13
  51.2 6.7 %collective-permute-start.12 = (bf16[256,4,128]{0,2,1:T(8,128)(2,1)S(1)}, bf16[256,4,128]{0,2,1:T(8,128)(2,1)S(1)}, u32[]{:S(2)}, u32[]{:S(2)}) collective-permute-start(bf16[256,4,128]{0,2,1:T(8,128)(2,1)S(1)} %add_convert_fusion.1), channel_id=1, source_target_pairs={{0,1},{1,2},{2,3},{3,4},{4,5},{5,6},{6,7},{7,8},{8,9},{9,10},{10,1... | collective-permute-start | bytes 786440 | tf_op jit(solution)/shard_map/ppermute | solution.py:15
  57.9 1.9 collective-permute-start.5
  59.9 4.1 collective-permute-start.4
  64.3 3.0 collective-permute-done.4
  67.3 0.5 multiply_convert_fusion
  67.9 0.5 fusion.12
  68.7 11.1 %collective-permute-start.13 = (bf16[256,4,128]{0,2,1:T(8,128)(2,1)S(1)}, bf16[256,4,128]{0,2,1:T(8,128)(2,1)S(1)}, u32[]{:S(2)}, u32[]{:S(2)}) collective-permute-start(bf16[256,4,128]{0,2,1:T(8,128)(2,1)S(1)} %add_convert_fusion), channel_id=1, source_target_pairs={{0,61},{1,62},{2,63},{3,0},{4,1},{5,2},{6,3},{7,4},{8,5},{9,6},{10... | collective-permute-start | bytes 786440 | tf_op jit(solution)/shard_map/ppermute | solution.py:15
  80.2 3.0 collective-permute-done.13
  83.2 2.7 convolution_bitcast_fusion
  85.9 2.1 fusion.18
  88.0 1.9 collective-permute-start.6
  90.0 1.4 fusion.44
  91.4 2.2 collective-permute-done.6
  93.6 1.3 add_convert_fusion.5
  94.9 6.9 %collective-permute-start.7 = (bf16[256,4,128]{2,0,1:T(8,128)(2,1)S(1)}, bf16[256,4,128]{2,0,1:T(8,128)(2,1)S(1)}, u32[]{:S(2)}, u32[]{:S(2)}) collective-permute-start(bf16[256,4,128]{2,0,1:T(8,128)(2,1)S(1)} %add_convert_fusion.5), channel_id=1, source_target_pairs={{0,1},{1,2},{2,3},{3,4},{4,5},{5,6},{6,7},{7,8},{8,9},{9,10},{10,1... | collective-permute-start | bytes 786440 | tf_op jit(solution)/shard_map/ppermute | solution.py:15
  102.5 2.6 collective-permute-done.7
  105.2 6.8 %collective-permute-start.8 = (bf16[256,4,128]{2,0,1:T(8,128)(2,1)S(1)}, bf16[256,4,128]{2,0,1:T(8,128)(2,1)S(1)}, u32[]{:S(2)}, u32[]{:S(2)}) collective-permute-start(bf16[256,4,128]{2,0,1:T(8,128)(2,1)S(1)} %add_convert_fusion.4), channel_id=1, source_target_pairs={{0,1},{1,2},{2,3},{3,4},{4,5},{5,6},{6,7},{7,8},{8,9},{9,10},{10,1... | collective-permute-start | bytes 786440 | tf_op jit(solution)/shard_map/ppermute | solution.py:15
  112.6 2.7 collective-permute-done.8
  115.3 0.8 add_convert_fusion.3
  116.1 14.5 %collective-permute-start.9 = (bf16[256,4,128]{2,0,1:T(8,128)(2,1)}, bf16[256,4,128]{2,0,1:T(8,128)(2,1)S(1)}, u32[]{:S(2)}, u32[]{:S(2)}) collective-permute-start(bf16[256,4,128]{2,0,1:T(8,128)(2,1)} %add_convert_fusion.3), channel_id=1, source_target_pairs={{0,61},{1,62},{2,63},{3,0},{4,1},{5,2},{6,3},{7,4},{8,5},{9,6},{10... | collective-permute-start | bytes 786440 | tf_op jit(solution)/shard_map/ppermute | solution.py:15
  130.9 0.8 copy.117
  131.8 8.2 %collective-permute-done.9 = bf16[256,4,128]{2,0,1:T(8,128)(2,1)S(1)} collective-permute-done((bf16[256,4,128]{2,0,1:T(8,128)(2,1)}, bf16[256,4,128]{2,0,1:T(8,128)(2,1)S(1)}, u32[]{:S(2)}, u32[]{:S(2)}) %collective-permute-start.9) | collective-permute-done | bytes 262176 | tf_op jit(solution)/shard_map/ppermute | solution.py:15
  140.2 0.8 copy.118
  141.0 156.0 %all-reduce.3.cloned.1.call-done = f32[1024,1024]{0,1:T(8,128)} async-done(((f32[1024,1024]{0,1:T(8,128)}), f32[1024,1024]{0,1:T(8,128)}) %all-reduce.3.cloned.1.call-update) | async-done | bytes 4194320 | tf_op jit(solution)/shard_map/psum | solution.py:105
  297.0 297.8 %all-reduce.4 = bf16[1024,1024]{0,1:T(8,128)(2,1)S(1)} all-reduce(f32[1024,1024]{0,1:T(8,128)} %all-reduce.3.cloned.1.call-done), channel_id=1, replica_groups=mesh['dp'=8,'ctx'=64] {'ctx'}, use_global_device_ids=true, to_apply=%region_10.11 | all-reduce | flops 1048576 | bytes 6291456 | tf_op jit(solution)/shard_map/psum | solution.py:106
  595.0 0.7 copy.120
  595.7 0.7 copy.119
  (60 shorter events, 5.4 us)
Async XLA Ops:
  7.2 6.2 %copy-start = (bf16[1024,512]{1,0:T(8,128)(2,1)S(1)}, bf16[1024,512]{1,0:T(8,128)(2,1)}, u32[]{:S(2)}) copy-start(bf16[1024,512]{1,0:T(8,128)(2,1)} %param.10) | copy-start | bytes 3145732
  7.2 289.8 %all-reduce.3.cloned.1.call-start = ((), (), s32[]{:S(2)}) async-start(), calls=%async_computation | async-start | bytes 8388608 | tf_op jit(solution)/shard_map/psum | solution.py:105
  8.4 16.7 %copy-start.2 = (bf16[1,256,512]{1,2,0:T(8,128)(2,1)}, bf16[1,256,512]{1,2,0:T(8,128)(2,1)S(1)}, u32[]{:S(2)}) copy-start(bf16[1,256,512]{1,2,0:T(8,128)(2,1)S(1)} %copy.87) | copy-start | bytes 786436
  8.4 23.5 %collective-permute-start.1 = (bf16[256,4,128]{0,2,1:T(8,128)(2,1)S(1)}, bf16[256,4,128]{0,2,1:T(8,128)(2,1)S(1)}, u32[]{:S(2)}, u32[]{:S(2)}) collective-permute-start(bf16[256,4,128]{0,2,1:T(8,128)(2,1)S(1)} %bitcast.101), channel_id=1, source_target_pairs={{0,1},{1,2},{2,3},{3,4},{4,5},{5,6},{6,7},{7,8},{8,9},{9,10},{10,1... | collective-permute-start | bytes 786440 | tf_op jit(solution)/shard_map/ppermute | solution.py:15
  15.6 14.8 %collective-permute-start = (bf16[256,4,128]{2,0,1:T(8,128)(2,1)}, bf16[256,4,128]{2,0,1:T(8,128)(2,1)}, u32[]{:S(2)}, u32[]{:S(2)}) collective-permute-start(bf16[256,4,128]{2,0,1:T(8,128)(2,1)} %bitcast.88), channel_id=1, source_target_pairs={{0,1},{1,2},{2,3},{3,4},{4,5},{5,6},{6,7},{7,8},{8,9},{9,10},{10,1... | collective-permute-start | bytes 786440 | tf_op jit(solution)/shard_map/ppermute | solution.py:15
  25.9 7.4 %collective-permute-start.10 = (bf16[256,4,128]{0,2,1:T(8,128)(2,1)S(1)}, bf16[256,4,128]{0,2,1:T(8,128)(2,1)S(1)}, u32[]{:S(2)}, u32[]{:S(2)}) collective-permute-start(bf16[256,4,128]{0,2,1:T(8,128)(2,1)S(1)} %fusion.19), channel_id=1, source_target_pairs={{0,1},{1,2},{2,3},{3,4},{4,5},{5,6},{6,7},{7,8},{8,9},{9,10},{10,1... | collective-permute-start | bytes 786440 | tf_op jit(solution)/shard_map/ppermute | solution.py:15
  31.9 15.6 %copy-start.4 = (bf16[256,4,128]{0,2,1:T(8,128)(2,1)}, bf16[256,4,128]{0,2,1:T(8,128)(2,1)S(1)}, u32[]{:S(2)}) copy-start(bf16[256,4,128]{0,2,1:T(8,128)(2,1)S(1)} %collective-permute-done.1) | copy-start | bytes 786436
  33.6 17.6 %collective-permute-start.11 = (bf16[256,4,128]{0,2,1:T(8,128)(2,1)S(1)}, bf16[256,4,128]{0,2,1:T(8,128)(2,1)S(1)}, u32[]{:S(2)}, u32[]{:S(2)}) collective-permute-start(bf16[256,4,128]{0,2,1:T(8,128)(2,1)S(1)} %add_convert_fusion.2), channel_id=1, source_target_pairs={{0,1},{1,2},{2,3},{3,4},{4,5},{5,6},{6,7},{7,8},{8,9},{9,10},{10,1... | collective-permute-start | bytes 786440 | tf_op jit(solution)/shard_map/ppermute | solution.py:15
  40.4 10.0 %collective-permute-start.3 = (bf16[256,4,128]{0,2,1:T(8,128)(2,1)S(1)}, bf16[256,4,128]{0,2,1:T(8,128)(2,1)S(1)}, u32[]{:S(2)}, u32[]{:S(2)}) collective-permute-start(bf16[256,4,128]{0,2,1:T(8,128)(2,1)S(1)} %collective-permute-done.1), channel_id=1, source_target_pairs={{0,1},{1,2},{2,3},{3,4},{4,5},{5,6},{6,7},{7,8},{8,9},{9,10},{10,1... | collective-permute-start | bytes 786440 | tf_op jit(solution)/shard_map/ppermute | solution.py:15
  42.3 7.5 %collective-permute-start.2 = (bf16[256,4,128]{2,0,1:T(8,128)(2,1)}, bf16[256,4,128]{2,0,1:T(8,128)(2,1)S(1)}, u32[]{:S(2)}, u32[]{:S(2)}) collective-permute-start(bf16[256,4,128]{2,0,1:T(8,128)(2,1)} %collective-permute-done), channel_id=1, source_target_pairs={{0,1},{1,2},{2,3},{3,4},{4,5},{5,6},{6,7},{7,8},{8,9},{9,10},{10,1... | collective-permute-start | bytes 786440 | tf_op jit(solution)/shard_map/ppermute | solution.py:15
  50.4 7.6 %copy-start.6 = (bf16[256,4,128]{0,2,1:T(8,128)(2,1)}, bf16[256,4,128]{0,2,1:T(8,128)(2,1)S(1)}, u32[]{:S(2)}) copy-start(bf16[256,4,128]{0,2,1:T(8,128)(2,1)S(1)} %collective-permute-done.3) | copy-start | bytes 786436
  51.2 17.4 %collective-permute-start.12 = (bf16[256,4,128]{0,2,1:T(8,128)(2,1)S(1)}, bf16[256,4,128]{0,2,1:T(8,128)(2,1)S(1)}, u32[]{:S(2)}, u32[]{:S(2)}) collective-permute-start(bf16[256,4,128]{0,2,1:T(8,128)(2,1)S(1)} %add_convert_fusion.1), channel_id=1, source_target_pairs={{0,1},{1,2},{2,3},{3,4},{4,5},{5,6},{6,7},{7,8},{8,9},{9,10},{10,1... | collective-permute-start | bytes 786440 | tf_op jit(solution)/shard_map/ppermute | solution.py:15
  57.9 9.9 %collective-permute-start.5 = (bf16[256,4,128]{0,2,1:T(8,128)(2,1)S(1)}, bf16[256,4,128]{0,2,1:T(8,128)(2,1)S(1)}, u32[]{:S(2)}, u32[]{:S(2)}) collective-permute-start(bf16[256,4,128]{0,2,1:T(8,128)(2,1)S(1)} %collective-permute-done.3), channel_id=1, source_target_pairs={{0,1},{1,2},{2,3},{3,4},{4,5},{5,6},{6,7},{7,8},{8,9},{9,10},{10,1... | collective-permute-start | bytes 786440 | tf_op jit(solution)/shard_map/ppermute | solution.py:15
  59.9 7.4 %collective-permute-start.4 = (bf16[256,4,128]{2,0,1:T(8,128)(2,1)S(1)}, bf16[256,4,128]{2,0,1:T(8,128)(2,1)S(1)}, u32[]{:S(2)}, u32[]{:S(2)}) collective-permute-start(bf16[256,4,128]{2,0,1:T(8,128)(2,1)S(1)} %collective-permute-done.2), channel_id=1, source_target_pairs={{0,1},{1,2},{2,3},{3,4},{4,5},{5,6},{6,7},{7,8},{8,9},{9,10},{10,1... | collective-permute-start | bytes 786440 | tf_op jit(solution)/shard_map/ppermute | solution.py:15
  67.9 0.8 copy-start.8
  67.9 15.3 %copy-start.1 = (bf16[1,256,1024]{2,1,0:T(8,128)(2,1)S(1)}, bf16[1,256,1024]{2,1,0:T(8,128)(2,1)}, u32[]{:S(2)}) copy-start(bf16[1,256,1024]{2,1,0:T(8,128)(2,1)} %param.8) | copy-start | bytes 1572868
  68.7 14.4 %collective-permute-start.13 = (bf16[256,4,128]{0,2,1:T(8,128)(2,1)S(1)}, bf16[256,4,128]{0,2,1:T(8,128)(2,1)S(1)}, u32[]{:S(2)}, u32[]{:S(2)}) collective-permute-start(bf16[256,4,128]{0,2,1:T(8,128)(2,1)S(1)} %add_convert_fusion), channel_id=1, source_target_pairs={{0,61},{1,62},{2,63},{3,0},{4,1},{5,2},{6,3},{7,4},{8,5},{9,6},{10... | collective-permute-start | bytes 786440 | tf_op jit(solution)/shard_map/ppermute | solution.py:15
  85.9 4.1 copy-start.3
  85.9 15.9 %copy-start.5 = (bf16[256,4,128]{0,2,1:T(8,128)(2,1)S(1)}, bf16[256,4,128]{0,2,1:T(8,128)(2,1)}, u32[]{:S(2)}) copy-start(bf16[256,4,128]{0,2,1:T(8,128)(2,1)} %copy-done.4) | copy-start | bytes 786436
  88.0 5.5 collective-permute-start.6
  90.0 22.0 %copy-start.7 = (bf16[256,4,128]{0,2,1:T(8,128)(2,1)S(1)}, bf16[256,4,128]{0,2,1:T(8,128)(2,1)}, u32[]{:S(2)}) copy-start(bf16[256,4,128]{0,2,1:T(8,128)(2,1)} %copy-done.6) | copy-start | bytes 786436
  94.9 35.8 %copy-start.9 = (bf16[256,4,128]{0,2,1:T(8,128)(2,1)S(1)}, bf16[256,4,128]{0,2,1:T(8,128)(2,1)}, u32[]{:S(2)}) copy-start(bf16[256,4,128]{0,2,1:T(8,128)(2,1)} %copy-done.8) | copy-start | bytes 786436
  94.9 10.2 %collective-permute-start.7 = (bf16[256,4,128]{2,0,1:T(8,128)(2,1)S(1)}, bf16[256,4,128]{2,0,1:T(8,128)(2,1)S(1)}, u32[]{:S(2)}, u32[]{:S(2)}) collective-permute-start(bf16[256,4,128]{2,0,1:T(8,128)(2,1)S(1)} %add_convert_fusion.5), channel_id=1, source_target_pairs={{0,1},{1,2},{2,3},{3,4},{4,5},{5,6},{6,7},{7,8},{8,9},{9,10},{10,1... | collective-permute-start | bytes 786440 | tf_op jit(solution)/shard_map/ppermute | solution.py:15
  105.2 10.1 %collective-permute-start.8 = (bf16[256,4,128]{2,0,1:T(8,128)(2,1)S(1)}, bf16[256,4,128]{2,0,1:T(8,128)(2,1)S(1)}, u32[]{:S(2)}, u32[]{:S(2)}) collective-permute-start(bf16[256,4,128]{2,0,1:T(8,128)(2,1)S(1)} %add_convert_fusion.4), channel_id=1, source_target_pairs={{0,1},{1,2},{2,3},{3,4},{4,5},{5,6},{6,7},{7,8},{8,9},{9,10},{10,1... | collective-permute-start | bytes 786440 | tf_op jit(solution)/shard_map/ppermute | solution.py:15
  116.1 23.9 %collective-permute-start.9 = (bf16[256,4,128]{2,0,1:T(8,128)(2,1)}, bf16[256,4,128]{2,0,1:T(8,128)(2,1)S(1)}, u32[]{:S(2)}, u32[]{:S(2)}) collective-permute-start(bf16[256,4,128]{2,0,1:T(8,128)(2,1)} %add_convert_fusion.3), channel_id=1, source_target_pairs={{0,61},{1,62},{2,63},{3,0},{4,1},{5,2},{6,3},{7,4},{8,5},{9,6},{10... | collective-permute-start | bytes 786440 | tf_op jit(solution)/shard_map/ppermute | solution.py:15
Sparse Core Ops, SparseCore 0:
  86.0 210.9 all-reduce.2
